TPU v7x, 128 devices: a whole 4x4x4 slice. The times are simulated.
128 devices in a mesh: thinker: 4 (over z), seq: 32 (over y, x, core).
Axes of the slice: x: 4, y: 4, z: 4, core: 2. Of those that a mesh axis runs over, the one named last changes fastest.
Arguments:
- queries: bfloat16 [4, 4096, 2048], P('thinker', 'seq'), may hold values from -6 to 6
- keys: bfloat16 [4, 4096, 512], P('thinker', 'seq'), may hold values from -6 to 6
- values: bfloat16 [4, 4096, 512], P('thinker', 'seq'), may hold values from -6 to 6
- forward_out: bfloat16 [4, 4096, 2048], P('thinker', 'seq'), may hold values from -2 to 2
- logsumexp: float32 [4, 16, 4096], P('thinker', None, 'seq'), may hold values from -1 to 16, as said below
- upstream: bfloat16 [128, 128, 2048], P(None, ('thinker', 'seq')), may hold values from -6 to 6
- lengths: int32 [4], replicated, may hold values from 512 to 4096, as said below
- sibling_mask: int32 [4, 3, 32], P('thinker', None, 'seq'), may hold values from 0 to 1, as said below
Outputs:
- query_grad: bfloat16 [4, 4096, 2048], P('thinker', 'seq')
- key_grad: bfloat16 [4, 4096, 512], P('thinker', 'seq')
- value_grad: bfloat16 [4, 4096, 512], P('thinker', 'seq')
Inputs may be any that keep to these rules, and one draw needn't show every extreme that they name: lengths[t] valid positions stand at the start of thinker t's trace; two thinkers have exactly 4096, one exactly 512. sibling_mask[t, r, b] = 1 where query block b of thinker t reads the recent tokens of thinker (t + r + 1) % 4; the two thinkers of length 4096 read each other in the blocks of the last 128 positions. `logsumexp`: rows of positions past a trace's length carry arbitrary values.
All inputs are finite; a program needn't handle non-finite values.
Results may differ from a plain program's by a relative error of at most 0.014.
Values may be sent and summed in bfloat16 or wider, within the bound.
No kernel may reach another device: no remote copies, remote signals or barrier semaphores. Data moves between devices by JAX's collectives and lax.ppermute only.
A program may use at most 128 MiB of HBM per device.

v0:
```python
import math
import jax
import jax.numpy as jnp
from jax import lax
from jax.sharding import PartitionSpec as P

BLOCK = 128


def from_behind(block, axis, distance):
    devices = range(lax.axis_size(axis))
    route = [(i - distance, i) for i in devices if i - distance in devices]
    return lax.ppermute(block, axis, route)


def pair_grads(
    query_heads, upstream_heads, lse_heads, delta_heads, key_rows, value_rows, allowed, factor
):
    count = key_rows.shape[0]
    kv_heads = query_heads.shape[1]
    head_dim = query_heads.shape[3]
    key_heads = key_rows.reshape(count, kv_heads, head_dim)
    value_heads = value_rows.reshape(count, kv_heads, head_dim)
    scores = (
        jnp.einsum("ikgd,jkd->kgij", query_heads, key_heads, preferred_element_type=jnp.float32)
        * factor
    )
    probs = jnp.where(allowed, jnp.exp(scores - lse_heads[..., None]), 0.0)
    dprobs = jnp.einsum(
        "ikgd,jkd->kgij", upstream_heads, value_heads, preferred_element_type=jnp.float32
    )
    dscores = probs * (dprobs - delta_heads[..., None])
    probs_low = probs.astype(jnp.bfloat16)
    dscores_low = dscores.astype(jnp.bfloat16)
    value_part = jnp.einsum(
        "kgij,ikgd->jkd", probs_low, upstream_heads, preferred_element_type=jnp.float32
    )
    key_part = (
        jnp.einsum("kgij,ikgd->jkd", dscores_low, query_heads, preferred_element_type=jnp.float32)
        * factor
    )
    query_part = (
        jnp.einsum("kgij,jkd->ikgd", dscores_low, key_heads, preferred_element_type=jnp.float32)
        * factor
    )
    rows = query_heads.shape[0]
    return (
        query_part.reshape(rows, -1),
        key_part.reshape(count, -1),
        value_part.reshape(count, -1),
    )


def shards(queries, keys, values, forward_out, logsumexp, upstream, lengths, sibling_mask):
    thinkers = lax.axis_size("thinker")
    seq_count = lax.axis_size("seq")
    devices = thinkers * seq_count
    rows = queries.shape[1]
    qwidth = queries.shape[2]
    kwidth = keys.shape[2]
    heads = logsumexp.shape[1]
    head_dim = qwidth // heads
    kv_heads = kwidth // head_dim
    group = heads // kv_heads
    factor = head_dim ** (-0.5)
    thinker = lax.axis_index("thinker")
    shard = lax.axis_index("seq")
    length = rows * seq_count
    per_peer = rows // devices
    arranged = upstream.reshape(devices, per_peer, 1, qwidth)
    arrived = lax.all_to_all(arranged, ("thinker", "seq"), split_axis=0, concat_axis=2, tiled=True)
    grad_out = arrived.reshape(rows, qwidth)
    query_heads = queries[0].reshape(rows, kv_heads, group, head_dim)
    upstream_heads = grad_out.reshape(rows, kv_heads, group, head_dim)
    output_heads = forward_out[0].reshape(rows, kv_heads, group, head_dim)
    delta = jnp.sum(upstream_heads.astype(jnp.float32) * output_heads.astype(jnp.float32), axis=-1)
    delta_heads = jnp.transpose(delta, (1, 2, 0))
    lse_heads = logsumexp[0].reshape(kv_heads, group, rows)
    my_length = lengths[thinker]
    first_query = shard * rows
    query_pos = first_query + jnp.arange(rows, dtype=jnp.int32)
    query_live = query_pos < my_length

    def own_block(key_rows, value_rows, key_start):
        count = key_rows.shape[0]
        key_pos = key_start + jnp.arange(count, dtype=jnp.int32)
        allowed = (
            (key_pos[None, :] <= query_pos[:, None])
            & query_live[:, None]
            & (key_pos[None, :] < my_length)
        )
        return pair_grads(
            query_heads,
            upstream_heads,
            lse_heads,
            delta_heads,
            key_rows,
            value_rows,
            allowed,
            factor,
        )

    initial = (
        jnp.zeros((rows, qwidth), jnp.float32),
        jnp.zeros((length, kwidth), jnp.bfloat16),
        jnp.zeros((length, kwidth), jnp.bfloat16),
    )
    piece_keys = lax.all_gather(keys, "seq", axis=1, tiled=True)[0]
    piece_values = lax.all_gather(values, "seq", axis=1, tiled=True)[0]
    piece_rows = piece_keys.shape[0]
    sub_rows = math.gcd(piece_rows, 512)

    def one_block(position, inner):
        total, key_buffer, value_buffer = inner
        offset = position * sub_rows
        key_rows = lax.dynamic_slice_in_dim(piece_keys, offset, sub_rows, 0)
        value_rows = lax.dynamic_slice_in_dim(piece_values, offset, sub_rows, 0)
        query_part, key_part, value_part = own_block(key_rows, value_rows, offset)
        key_buffer = lax.dynamic_update_slice_in_dim(
            key_buffer, key_part.astype(jnp.bfloat16), offset, 0
        )
        value_buffer = lax.dynamic_update_slice_in_dim(
            value_buffer, value_part.astype(jnp.bfloat16), offset, 0
        )
        return (total + query_part, key_buffer, value_buffer)

    query_total, key_buffer, value_buffer = lax.fori_loop(
        0, piece_rows // sub_rows, one_block, initial
    )
    own_key, own_value = (
        lax.psum_scatter(key_buffer, "seq", scatter_dimension=0, tiled=True).astype(jnp.float32),
        lax.psum_scatter(value_buffer, "seq", scatter_dimension=0, tiled=True).astype(jnp.float32),
    )
    sibling_keys, sibling_values = (
        lax.all_gather(keys, "thinker", axis=0, tiled=True),
        lax.all_gather(values, "thinker", axis=0, tiled=True),
    )
    prior_keys, prior_values = from_behind((sibling_keys, sibling_values), "seq", 1)
    window_keys = jnp.roll(jnp.concatenate([prior_keys, sibling_keys], axis=1), -thinker, axis=0)
    window_values = jnp.roll(
        jnp.concatenate([prior_values, sibling_values], axis=1), -thinker, axis=0
    )
    key_pos = first_query - rows + jnp.arange(2 * rows, dtype=jnp.int32)
    near = (
        (key_pos[None, :] <= query_pos[:, None])
        & (key_pos[None, :] > query_pos[:, None] - rows)
        & (key_pos[None, :] >= 0)
        & query_live[:, None]
    )
    mask_rows = sibling_mask[0]
    key_terms_list = [jnp.zeros((2 * rows, kwidth), jnp.float32)]
    value_terms_list = [jnp.zeros((2 * rows, kwidth), jnp.float32)]
    for offset in range(1, thinkers):
        sibling = (thinker + offset) % thinkers
        visible = jnp.repeat(mask_rows[offset - 1], BLOCK) == 1
        allowed = near & visible[:, None] & (key_pos[None, :] < lengths[sibling])
        extra_query, extra_key, extra_value = pair_grads(
            query_heads,
            upstream_heads,
            lse_heads,
            delta_heads,
            window_keys[offset],
            window_values[offset],
            allowed,
            factor,
        )
        query_total = query_total + extra_query
        key_terms_list.append(extra_key)
        value_terms_list.append(extra_value)
    key_stack = jnp.roll(jnp.stack(key_terms_list), thinker, axis=0)
    value_stack = jnp.roll(jnp.stack(value_terms_list), thinker, axis=0)
    sibling_key, sibling_value = (
        lax.psum_scatter(
            key_stack.astype(jnp.bfloat16), "thinker", scatter_dimension=0, tiled=True
        ).astype(jnp.float32),
        lax.psum_scatter(
            value_stack.astype(jnp.bfloat16), "thinker", scatter_dimension=0, tiled=True
        ).astype(jnp.float32),
    )
    earlier_key, earlier_value = (
        from_behind(sibling_key[0, :rows].astype(jnp.bfloat16), "seq", -1).astype(jnp.float32),
        from_behind(sibling_value[0, :rows].astype(jnp.bfloat16), "seq", -1).astype(jnp.float32),
    )
    key_grad = (own_key + sibling_key[0, rows:] + earlier_key).astype(jnp.bfloat16)[None]
    value_grad = (own_value + sibling_value[0, rows:] + earlier_value).astype(jnp.bfloat16)[None]
    return (query_total.astype(jnp.bfloat16)[None], key_grad, value_grad)


def solution(mesh):
    placed = (
        P("thinker", "seq", None),
        P("thinker", "seq", None),
        P("thinker", "seq", None),
        P("thinker", "seq", None),
        P("thinker", None, "seq"),
        P(None, ("thinker", "seq"), None),
        P(),
        P("thinker", None, "seq"),
    )
    return jax.shard_map(
        shards,
        mesh=mesh,
        in_specs=placed,
        out_specs=(P("thinker", "seq", None), P("thinker", "seq", None), P("thinker", "seq", None)),
        check_vma=False,
    )
```

profile of v0, /device:TPU:0, one launch (start us, length us, event | category | flops | bytes accessed | tf_op | source)
XLA Modules:
  0.0 450.8 jit_solution(13187898375791302462)
XLA Ops:
  15.2 11.2 %all-to-all-start = ((bf16[128,2,1024]{2,1,0:T(2,128)(2,1)}), bf16[128,2,1024]{2,1,0:T(2,128)(2,1)S(1)}, u32[]{:S(2)}, u32[]{:S(2)}) async-start(bf16[128,2,1024]{2,1,0:T(2,128)(2,1)} %reshape.165), calls=%async_computation | async-start | bytes 1048576 | tf_op jit(solution)/shard_map/all_to_all | solution.py:71
  26.5 15.7 %all_gather.15 = bf16[4,128,512]{2,1,0:T(8,128)(2,1)S(1)} all-gather(bf16[1,128,512]{2,1,0:T(8,128)(2,1)S(1)} %copy-done.17), channel_id=1, replica_groups=mesh['thinker'=4,'seq'=32] {'thinker'}, dimensions={0}, use_global_device_ids=true | all-gather | bytes 655360 | tf_op jit(solution)/shard_map/all_gather | solution.py:136
  44.6 12.8 %all_gather.14 = bf16[4,128,512]{2,1,0:T(8,128)(2,1)S(1)} all-gather(bf16[1,128,512]{2,1,0:T(8,128)(2,1)S(1)} %copy-done.18), channel_id=1, replica_groups=mesh['thinker'=4,'seq'=32] {'thinker'}, dimensions={0}, use_global_device_ids=true | all-gather | bytes 655360 | tf_op jit(solution)/shard_map/all_gather | solution.py:135
  57.6 3.7 collective-permute-start
  104.4 3.3 fusion.36
  108.5 14.2 %all-gather.5.cloned.1.call-done = bf16[1,4096,512]{1,2,0:T(8,128)(2,1)} async-done(((bf16[1,128,512]{1,2,0:T(8,128)(2,1)}), bf16[1,4096,512]{1,2,0:T(8,128)(2,1)}) %all-gather.5.cloned.1.call-update) | async-done | bytes 4194320 | tf_op jit(solution)/shard_map/all_gather | solution.py:109
  127.2 147.3 %while.20 = (s32[]{:T(128)}, f32[128,2048]{0,1:T(8,128)}, bf16[4096,512]{1,0:T(8,128)(2,1)}, bf16[4096,512]{1,0:T(8,128)(2,1)}, bf16[4096,512]{0,1:T(8,128)(2,1)...) while((s32[]{:T(128)}, f32[128,2048]{0,1:T(8,128)}, ...), condition=%wide.region_2.3_spmd.clone.clone.clone, body=%wide.region_1.2_spmd.clone.clone.clone.sunk | while | flops 1354434432 | bytes 44792396 | solution.py:127
  132.7 2.8 fusion.147
  139.3 2.6 fusion.148
  151.2 2.8 fusion.147
  157.8 2.6 fusion.148
  169.6 2.8 fusion.147
  176.2 2.6 fusion.148
  188.0 2.8 fusion.147
  194.6 2.6 fusion.148
  206.4 2.8 fusion.147
  213.0 2.6 fusion.148
  224.8 2.8 fusion.147
  243.1 2.8 fusion.147
  249.8 2.6 fusion.148
  261.5 2.8 fusion.147
  287.9 2.7 fusion.69
  290.6 65.7 %reduce-scatter.9.cloned.1.call-done = bf16[128,512]{1,0:T(8,128)(2,1)} async-done(((bf16[4096,512]{1,0:T(8,128)(2,1)}), bf16[128,512]{1,0:T(8,128)(2,1)}) %reduce-scatter.9.cloned.1.call-update) | async-done | bytes 131088 | tf_op jit(solution)/shard_map/reduce_scatter | solution.py:132
  358.0 83.6 %reduce-scatter.5.cloned.1.call-done = bf16[128,512]{1,0:T(8,128)(2,1)} async-done(((bf16[4096,512]{1,0:T(8,128)(2,1)}), bf16[128,512]{1,0:T(8,128)(2,1)}) %reduce-scatter.5.cloned.1.call-update) | async-done | bytes 131088 | tf_op jit(solution)/shard_map/reduce_scatter | solution.py:131
  (285 shorter events, 180.7 us)
Async XLA Ops:
  8.0 18.5 %copy-start.17 = (bf16[1,128,512]{2,1,0:T(8,128)(2,1)S(1)}, bf16[1,128,512]{2,1,0:T(8,128)(2,1)}, u32[]{:S(2)}) copy-start(bf16[1,128,512]{2,1,0:T(8,128)(2,1)} %param.16) | copy-start | bytes 393220
  8.0 100.5 %all-gather.3.cloned.1.call-start = ((), (), s32[]{:S(2)}) async-start(), calls=%async_computation.5 | async-start | bytes 4325376 | tf_op jit(solution)/shard_map/all_gather | solution.py:108
  9.8 113.0 %all-gather.5.cloned.1.call-start = ((), (), s32[]{:S(2)}) async-start(), calls=%async_computation.6 | async-start | bytes 4325376 | tf_op jit(solution)/shard_map/all_gather | solution.py:109
  14.0 30.5 %copy-start.18 = (bf16[1,128,512]{2,1,0:T(8,128)(2,1)S(1)}, bf16[1,128,512]{2,1,0:T(8,128)(2,1)}, u32[]{:S(2)}) copy-start(bf16[1,128,512]{2,1,0:T(8,128)(2,1)} %param.15) | copy-start | bytes 393220
  15.2 46.2 %copy-start.22 = (s32[4]{0:T(128)S(1)}, s32[4]{0:T(128)}, u32[]{:S(2)}) copy-start(s32[4]{0:T(128)} %param.20) | copy-start | bytes 52
  15.2 46.8 %copy-start.23 = (s32[1,3,1]{1,2,0:T(1,128)S(1)}, s32[1,3,1]{1,2,0:T(1,128)}, u32[]{:S(2)}) copy-start(s32[1,3,1]{1,2,0:T(1,128)} %param.21) | copy-start | bytes 40
  15.2 50.7 %copy-start.19 = (bf16[1,128,2048]{2,1,0:T(8,128)(2,1)S(1)}, bf16[1,128,2048]{2,1,0:T(8,128)(2,1)}, u32[]{:S(2)}) copy-start(bf16[1,128,2048]{2,1,0:T(8,128)(2,1)} %param.14) | copy-start | bytes 1572868
  15.2 54.5 %all-to-all-start = ((bf16[128,2,1024]{2,1,0:T(2,128)(2,1)}), bf16[128,2,1024]{2,1,0:T(2,128)(2,1)S(1)}, u32[]{:S(2)}, u32[]{:S(2)}) async-start(bf16[128,2,1024]{2,1,0:T(2,128)(2,1)} %reshape.165), calls=%async_computation | async-start | bytes 1048576 | tf_op jit(solution)/shard_map/all_to_all | solution.py:71
  26.4 255.5 %reduce-scatter.11.cloned.1.call-start = ((), (), s32[]{:S(2)}) async-start(), calls=%async_computation.10 | async-start | bytes 1310720 | tf_op jit(solution)/shard_map/reduce_scatter | solution.py:176
  42.4 30.8 %collective-permute-start.1 = (bf16[4,128,512]{1,2,0:T(8,128)(2,1)S(1)}, bf16[4,128,512]{1,2,0:T(8,128)(2,1)}, u32[]{:S(2)}, u32[]{:S(2)}) collective-permute-start(bf16[4,128,512]{1,2,0:T(8,128)(2,1)S(1)} %copy.162), channel_id=1, source_target_pairs={{0,1},{1,2},{2,3},{3,4},{4,5},{5,6},{6,7},{7,8},{8,9},{9,10},{10,1... | collective-permute-start | bytes 1572872 | tf_op jit(solution)/shard_map/ppermute | solution.py:13
  57.6 15.6 %collective-permute-start = (bf16[4,128,512]{1,2,0:T(8,128)(2,1)S(1)}, bf16[4,128,512]{1,2,0:T(8,128)(2,1)}, u32[]{:S(2)}, u32[]{:S(2)}) collective-permute-start(bf16[4,128,512]{1,2,0:T(8,128)(2,1)S(1)} %copy.158), channel_id=1, source_target_pairs={{0,1},{1,2},{2,3},{3,4},{4,5},{5,6},{6,7},{7,8},{8,9},{9,10},{10,1... | collective-permute-start | bytes 1572872 | tf_op jit(solution)/shard_map/ppermute | solution.py:13
  73.2 3.9 copy-start.24
  107.7 176.6 %reduce-scatter.7.cloned.1.call-start = ((), (), s32[]{:S(2)}) async-start(), calls=%async_computation.8 | async-start | bytes 1310720 | tf_op jit(solution)/shard_map/reduce_scatter | solution.py:173
  108.2 248.1 %reduce-scatter.9.cloned.1.call-start = ((), (), s32[]{:S(2)}) async-start(), calls=%async_computation.9 | async-start | bytes 4325376 | tf_op jit(solution)/shard_map/reduce_scatter | solution.py:132
  274.6 166.9 %reduce-scatter.5.cloned.1.call-start = ((), (), s32[]{:S(2)}) async-start(), calls=%async_computation.7 | async-start | bytes 4325376 | tf_op jit(solution)/shard_map/reduce_scatter | solution.py:131
  277.6 2.7 copy-start.9
  277.6 2.7 copy-start.12
  280.3 6.2 %copy-start.2 = (f32[128,2048]{0,1:T(8,128)S(1)}, f32[128,2048]{0,1:T(8,128)}, u32[]{:S(2)}) copy-start(f32[128,2048]{0,1:T(8,128)} %get-tuple-element.221) | copy-start | bytes 3145732
  280.6 7.2 %copy-start.10 = (f32[128,2048]{1,0:T(8,128)S(1)}, f32[128,2048]{1,0:T(8,128)}, u32[]{:S(2)}) copy-start(f32[128,2048]{1,0:T(8,128)} %copy.174) | copy-start | bytes 3145732
  282.0 5.9 %copy-start.11 = (f32[128,2048]{1,0:T(8,128)S(1)}, f32[128,2048]{1,0:T(8,128)}, u32[]{:S(2)}) copy-start(f32[128,2048]{1,0:T(8,128)} %copy.168) | copy-start | bytes 3145732
  283.0 7.6 %collective-permute-start.3 = (bf16[128,512]{1,0:T(8,128)(2,1)S(1)}, bf16[128,512]{1,0:T(8,128)(2,1)}, u32[]{:S(2)}, u32[]{:S(2)}) collective-permute-start(bf16[128,512]{1,0:T(8,128)(2,1)S(1)} %slice_bitcast_fusion), channel_id=1, source_target_pairs={{1,0},{2,1},{3,2},{4,3},{5,4},{6,5},{7,6},{8,7},{9,8},{10,9},{11,1... | collective-permute-start | bytes 393224 | tf_op jit(solution)/shard_map/ppermute | solution.py:13
  285.2 72.8 %collective-permute-start.2 = (bf16[128,512]{1,0:T(8,128)(2,1)S(1)}, bf16[128,512]{1,0:T(8,128)(2,1)S(1)}, u32[]{:S(2)}, u32[]{:S(2)}) collective-permute-start(bf16[128,512]{1,0:T(8,128)(2,1)S(1)} %slice_bitcast_fusion.2), channel_id=1, source_target_pairs={{1,0},{2,1},{3,2},{4,3},{5,4},{6,5},{7,6},{8,7},{9,8},{10,9},{11,1... | collective-permute-start | bytes 393224 | tf_op jit(solution)/shard_map/ppermute | solution.py:13
  287.9 68.5 %copy-start.20 = (bf16[1,256,512]{2,1,0:T(8,128)(2,1)S(1)}, bf16[1,256,512]{2,1,0:T(8,128)(2,1)}, u32[]{:S(2)}) copy-start(bf16[1,256,512]{2,1,0:T(8,128)(2,1)} %reduce-scatter.11.cloned.1.call-done) | copy-start | bytes 786436
  287.9 153.7 %copy-start.21 = (bf16[1,256,512]{2,1,0:T(8,128)(2,1)S(1)}, bf16[1,256,512]{2,1,0:T(8,128)(2,1)}, u32[]{:S(2)}) copy-start(bf16[1,256,512]{2,1,0:T(8,128)(2,1)} %reduce-scatter.7.cloned.1.call-done) | copy-start | bytes 786436
  (33 other events, 38.8 us)
Sparse Core Ops, SparseCore 0:
  11.6 57.4 all-gather.2
  71.8 50.8 all-gather.4
Sparse Core Ops, SparseCore 1:
  107.7 24.0 reduce-scatter.10
  134.1 23.7 reduce-scatter.6
  274.7 81.6 reduce-scatter.8
  360.0 81.5 reduce-scatter.4
where the time goes:
time: 455 us; the launch traced here: 451 us
  waiting for transfers between devices  165 us (36%)
  matrix products  104 us (23%)
  local copies, waits for them, and re-layouts  83.9 us (18%)
  other arithmetic  30.5 us (7%)
  blocking collectives  28.5 us (6%)
  starting transfers between devices  20.1 us (4%)
  between operations  18.1 us (4%)
    reduce_scatter x1, waiting for transfers between devices, shards(): lax.psum_scatter(key_buffer, 'seq', scatter_dimension=0, tiled=True)  83.6 us
    reduce_scatter x1, waiting for transfers between devices, shards(): lax.psum_scatter(value_buffer, 'seq', scatter_dimension=0, tiled=True)  65.7 us
    dot_general x11, matrix products, pair_grads(): jnp.einsum('kgij,ikgd->jkd', probs_low, upstream_heads, preferred_element...  28.6 us
    dot_general x11, matrix products, pair_grads(): jnp.einsum('kgij,ikgd->jkd', dscores_low, query_heads, preferred_element_...  25.7 us
    dot_general x11, matrix products, pair_grads(): jnp.einsum('ikgd,jkd->kgij', upstream_heads, value_heads, preferred_eleme...  25 us
    dot_general x11, matrix products, pair_grads(): jnp.einsum('ikgd,jkd->kgij', query_heads, key_heads, preferred_element_ty...  19.4 us
    dynamic_update_slice x16, local copies, waits for them, and re-layouts, one_block(): lax.dynamic_update_slice_in_dim(value_buffer, value_part.astype(jnp.bfloa...  18.4 us
    all_gather x1, blocking collectives, shards(): lax.all_gather(values, 'thinker', axis=0, tiled=True)  15.7 us
  transfers between devices with their start and end apart: 11, of which 3 were waited for; matrix products, arithmetic and copies ran while one was open for 44% of the time, Pallas kernels for 0%

commit v1 on v0

--- a/solution.py
+++ b/solution.py
@@ -133,7 +133,9 @@
     )
     sibling_keys, sibling_values = (
         lax.all_gather(keys, "thinker", axis=0, tiled=True),
-        lax.all_gather(values, "thinker", axis=0, tiled=True),
+        jnp.concatenate(
+            lax.all_to_all(jnp.stack([values] * lax.axis_size("thinker")), "thinker", 0, 0), axis=0
+        ),
     )
     prior_keys, prior_values = from_behind((sibling_keys, sibling_values), "seq", 1)
     window_keys = jnp.roll(jnp.concatenate([prior_keys, sibling_keys], axis=1), -thinker, axis=0)

time: 455 us -> 456 us (level)
  blocking collectives: 28.5 us -> 17.8 us
  waiting for transfers between devices: 165 us -> 173 us
    all_gather x1 -> x0, blocking collectives: 15.7 us -> none  [shards(): lax.all_gather(values, 'thinker', axis=0, tiled=True)]
    all_to_all x1, waiting for transfers between devices: 0.01 us -> 6.22 us  [shards(): lax.all_to_all(arranged, ('thinker', 'seq'), split_axis=0, concat_axis=2,...]
    all_to_all x0 -> x1, starting transfers between devices: none -> 5.42 us  [shards(): lax.all_to_all(jnp.stack([values] * lax.axis_size('thinker')), 'thinker',...]
    all_gather x1, blocking collectives: 12.8 us -> 17.8 us  [shards(): lax.all_gather(keys, 'thinker', axis=0, tiled=True)]
  transfers between devices with their start and end apart: 11 -> 12, of which waited for: 3 -> 4; matrix products, arithmetic and copies ran while one was open for 44% -> 44% of each run, Pallas kernels for 0% -> 0%
where the time goes in v1:
time: 456 us; the launch traced here: 452 us
  waiting for transfers between devices  173 us (38%)
  matrix products  104 us (23%)
  local copies, waits for them, and re-layouts  85.4 us (19%)
  other arithmetic  30.9 us (7%)
  starting transfers between devices  22 us (5%)
  between operations  18.1 us (4%)
  blocking collectives  17.8 us (4%)
    reduce_scatter x1, waiting for transfers between devices, shards(): lax.psum_scatter(key_buffer, 'seq', scatter_dimension=0, tiled=True)  83.6 us
    reduce_scatter x1, waiting for transfers between devices, shards(): lax.psum_scatter(value_buffer, 'seq', scatter_dimension=0, tiled=True)  65.9 us
    dot_general x11, matrix products, pair_grads(): jnp.einsum('kgij,ikgd->jkd', probs_low, upstream_heads, preferred_element...  28.6 us
    dot_general x11, matrix products, pair_grads(): jnp.einsum('kgij,ikgd->jkd', dscores_low, query_heads, preferred_element_...  25.8 us
    dot_general x11, matrix products, pair_grads(): jnp.einsum('ikgd,jkd->kgij', upstream_heads, value_heads, preferred_eleme...  25 us
    dot_general x11, matrix products, pair_grads(): jnp.einsum('ikgd,jkd->kgij', query_heads, key_heads, preferred_element_ty...  19.4 us
    dynamic_update_slice x16, local copies, waits for them, and re-layouts, one_block(): lax.dynamic_update_slice_in_dim(value_buffer, value_part.astype(jnp.bfloa...  18.4 us
    all_gather x1, blocking collectives, shards(): lax.all_gather(keys, 'thinker', axis=0, tiled=True)  17.8 us
  transfers between devices with their start and end apart: 12, of which 4 were waited for; matrix products, arithmetic and copies ran while one was open for 44% of the time, Pallas kernels for 0%

profile of v1, /device:TPU:0, one launch (start us, length us, event | category | flops | bytes accessed | tf_op | source)
XLA Modules:
  0.0 451.9 jit_solution(16360508699661933878)
XLA Ops:
  13.5 5.4 %all-to-all-start.1 = ((bf16[4,1,128,512]{2,3,1,0:T(8,128)(2,1)}), bf16[4,1,128,512]{2,3,1,0:T(8,128)(2,1)S(1)}, u32[]{:S(2)}, u32[]{:S(2)}) async-start(bf16[4,1,128,512]{2,3,1,0:T(8,128)(2,1)} %stack.6), calls=%async_computation.1 | async-start | bytes 1048576 | tf_op jit(solution)/shard_map/all_to_all | solution.py:137
  18.9 17.8 %all_gather.11 = bf16[4,128,512]{2,1,0:T(8,128)(2,1)S(1)} all-gather(bf16[1,128,512]{2,1,0:T(8,128)(2,1)S(1)} %copy-done.17), channel_id=1, replica_groups=mesh['thinker'=4,'seq'=32] {'thinker'}, dimensions={0}, use_global_device_ids=true | all-gather | bytes 655360 | tf_op jit(solution)/shard_map/all_gather | solution.py:135
  43.2 9.2 %all-to-all-start = ((bf16[128,2,1024]{2,1,0:T(2,128)(2,1)}), bf16[128,2,1024]{2,1,0:T(2,128)(2,1)S(1)}, u32[]{:S(2)}, u32[]{:S(2)}) async-start(bf16[128,2,1024]{2,1,0:T(2,128)(2,1)} %reshape.172), calls=%async_computation | async-start | bytes 1048576 | tf_op jit(solution)/shard_map/all_to_all | solution.py:71
  61.7 6.2 %all-to-all-done = bf16[128,2,1024]{2,1,0:T(2,128)(2,1)S(1)} async-done(((bf16[128,2,1024]{2,1,0:T(2,128)(2,1)}), bf16[128,2,1024]{2,1,0:T(2,128)(2,1)S(1)}, u32[]{:S(2)}, u32[]{:S(2)}) %all-to-all-start) | async-done | bytes 524320 | tf_op jit(solution)/shard_map/all_to_all | solution.py:71
  102.5 3.3 fusion.36
  106.6 15.9 %all-gather.5.cloned.1.call-done = bf16[1,4096,512]{1,2,0:T(8,128)(2,1)} async-done(((bf16[1,128,512]{1,2,0:T(8,128)(2,1)}), bf16[1,4096,512]{1,2,0:T(8,128)(2,1)}) %all-gather.5.cloned.1.call-update) | async-done | bytes 4194320 | tf_op jit(solution)/shard_map/all_gather | solution.py:109
  127.1 148.5 %while.20 = (s32[]{:T(128)}, f32[128,2048]{0,1:T(8,128)}, bf16[4096,512]{1,0:T(8,128)(2,1)}, bf16[4096,512]{1,0:T(8,128)(2,1)}, bf16[4096,512]{0,1:T(8,128)(2,1)...) while((s32[]{:T(128)}, f32[128,2048]{0,1:T(8,128)}, ...), condition=%wide.region_2.3_spmd.clone.clone.clone, body=%wide.region_1.2_spmd.clone.clone.clone.sunk | while | flops 1354434432 | bytes 44792396 | solution.py:127
  132.7 2.8 fusion.147
  139.3 2.6 fusion.148
  151.3 2.8 fusion.147
  157.9 2.6 fusion.148
  169.8 2.8 fusion.147
  176.4 2.6 fusion.148
  188.3 2.8 fusion.147
  195.0 2.6 fusion.148
  206.9 2.8 fusion.147
  213.5 2.6 fusion.148
  225.4 2.8 fusion.147
  244.0 2.8 fusion.147
  262.5 2.8 fusion.147
  269.1 2.6 fusion.148
  288.8 2.7 fusion.69
  291.5 65.9 %reduce-scatter.9.cloned.1.call-done = bf16[128,512]{1,0:T(8,128)(2,1)} async-done(((bf16[4096,512]{1,0:T(8,128)(2,1)}), bf16[128,512]{1,0:T(8,128)(2,1)}) %reduce-scatter.9.cloned.1.call-update) | async-done | bytes 131088 | tf_op jit(solution)/shard_map/reduce_scatter | solution.py:132
  359.1 83.6 %reduce-scatter.5.cloned.1.call-done = bf16[128,512]{1,0:T(8,128)(2,1)} async-done(((bf16[4096,512]{1,0:T(8,128)(2,1)}), bf16[128,512]{1,0:T(8,128)(2,1)}) %reduce-scatter.5.cloned.1.call-update) | async-done | bytes 131088 | tf_op jit(solution)/shard_map/reduce_scatter | solution.py:131
  (287 shorter events, 184.7 us)
Async XLA Ops:
  8.0 10.9 %copy-start.17 = (bf16[1,128,512]{2,1,0:T(8,128)(2,1)S(1)}, bf16[1,128,512]{2,1,0:T(8,128)(2,1)}, u32[]{:S(2)}) copy-start(bf16[1,128,512]{2,1,0:T(8,128)(2,1)} %param.15) | copy-start | bytes 393220
  8.0 98.6 %all-gather.3.cloned.1.call-start = ((), (), s32[]{:S(2)}) async-start(), calls=%async_computation.6 | async-start | bytes 4325376 | tf_op jit(solution)/shard_map/all_gather | solution.py:108
  9.8 29.9 %copy-start.19 = (bf16[128,1,2048]{2,0,1:T(8,128)(2,1)S(1)}, bf16[128,1,2048]{2,0,1:T(8,128)(2,1)}, u32[]{:S(2)}) copy-start(bf16[128,1,2048]{2,0,1:T(8,128)(2,1)} %param.19) | copy-start | bytes 1572868
  9.8 112.8 %all-gather.5.cloned.1.call-start = ((), (), s32[]{:S(2)}) async-start(), calls=%async_computation.7 | async-start | bytes 4325376 | tf_op jit(solution)/shard_map/all_gather | solution.py:109
  13.5 29.7 %all-to-all-start.1 = ((bf16[4,1,128,512]{2,3,1,0:T(8,128)(2,1)}), bf16[4,1,128,512]{2,3,1,0:T(8,128)(2,1)S(1)}, u32[]{:S(2)}, u32[]{:S(2)}) async-start(bf16[4,1,128,512]{2,3,1,0:T(8,128)(2,1)} %stack.6), calls=%async_computation.1 | async-start | bytes 1048576 | tf_op jit(solution)/shard_map/all_to_all | solution.py:137
  18.9 23.0 %copy-start.22 = (s32[4]{0:T(128)S(1)}, s32[4]{0:T(128)}, u32[]{:S(2)}) copy-start(s32[4]{0:T(128)} %param.20) | copy-start | bytes 52
  18.9 23.6 %copy-start.23 = (s32[1,3,1]{1,2,0:T(1,128)S(1)}, s32[1,3,1]{1,2,0:T(1,128)}, u32[]{:S(2)}) copy-start(s32[1,3,1]{1,2,0:T(1,128)} %param.21) | copy-start | bytes 40
  36.7 21.2 %copy-start.18 = (bf16[1,128,2048]{2,1,0:T(8,128)(2,1)S(1)}, bf16[1,128,2048]{2,1,0:T(8,128)(2,1)}, u32[]{:S(2)}) copy-start(bf16[1,128,2048]{2,1,0:T(8,128)(2,1)} %param.14) | copy-start | bytes 1572868
  37.0 34.4 %collective-permute-start = (bf16[4,128,512]{1,2,0:T(8,128)(2,1)S(1)}, bf16[4,128,512]{1,2,0:T(8,128)(2,1)}, u32[]{:S(2)}, u32[]{:S(2)}) collective-permute-start(bf16[4,128,512]{1,2,0:T(8,128)(2,1)S(1)} %copy.157), channel_id=1, source_target_pairs={{0,1},{1,2},{2,3},{3,4},{4,5},{5,6},{6,7},{7,8},{8,9},{9,10},{10,1... | collective-permute-start | bytes 1572872 | tf_op jit(solution)/shard_map/ppermute | solution.py:13
  43.2 24.7 %all-to-all-start = ((bf16[128,2,1024]{2,1,0:T(2,128)(2,1)}), bf16[128,2,1024]{2,1,0:T(2,128)(2,1)S(1)}, u32[]{:S(2)}, u32[]{:S(2)}) async-start(bf16[128,2,1024]{2,1,0:T(2,128)(2,1)} %reshape.172), calls=%async_computation | async-start | bytes 1048576 | tf_op jit(solution)/shard_map/all_to_all | solution.py:71
  52.4 230.5 %reduce-scatter.11.cloned.1.call-start = ((), (), s32[]{:S(2)}) async-start(), calls=%async_computation.11 | async-start | bytes 1310720 | tf_op jit(solution)/shard_map/reduce_scatter | solution.py:178
  53.1 18.3 %collective-permute-start.1 = (bf16[4,128,512]{1,2,0:T(8,128)(2,1)S(1)}, bf16[4,128,512]{1,2,0:T(8,128)(2,1)}, u32[]{:S(2)}, u32[]{:S(2)}) collective-permute-start(bf16[4,128,512]{1,2,0:T(8,128)(2,1)S(1)} %bitcast.305), channel_id=1, source_target_pairs={{0,1},{1,2},{2,3},{3,4},{4,5},{5,6},{6,7},{7,8},{8,9},{9,10},{10,1... | collective-permute-start | bytes 1572872 | tf_op jit(solution)/shard_map/ppermute | solution.py:13
  71.4 3.9 copy-start.24
  105.8 179.4 %reduce-scatter.7.cloned.1.call-start = ((), (), s32[]{:S(2)}) async-start(), calls=%async_computation.9 | async-start | bytes 1310720 | tf_op jit(solution)/shard_map/reduce_scatter | solution.py:175
  106.4 251.0 %reduce-scatter.9.cloned.1.call-start = ((), (), s32[]{:S(2)}) async-start(), calls=%async_computation.10 | async-start | bytes 4325376 | tf_op jit(solution)/shard_map/reduce_scatter | solution.py:132
  275.5 167.1 %reduce-scatter.5.cloned.1.call-start = ((), (), s32[]{:S(2)}) async-start(), calls=%async_computation.8 | async-start | bytes 4325376 | tf_op jit(solution)/shard_map/reduce_scatter | solution.py:131
  278.5 2.7 copy-start.12
  281.2 6.2 %copy-start.2 = (f32[128,2048]{0,1:T(8,128)S(1)}, f32[128,2048]{0,1:T(8,128)}, u32[]{:S(2)}) copy-start(f32[128,2048]{0,1:T(8,128)} %get-tuple-element.221) | copy-start | bytes 3145732
  281.5 7.2 %copy-start.10 = (f32[128,2048]{1,0:T(8,128)S(1)}, f32[128,2048]{1,0:T(8,128)}, u32[]{:S(2)}) copy-start(f32[128,2048]{1,0:T(8,128)} %copy.172) | copy-start | bytes 3145732
  282.9 5.9 %copy-start.11 = (f32[128,2048]{1,0:T(8,128)S(1)}, f32[128,2048]{1,0:T(8,128)}, u32[]{:S(2)}) copy-start(f32[128,2048]{1,0:T(8,128)} %copy.166) | copy-start | bytes 3145732
  283.9 7.6 %collective-permute-start.3 = (bf16[128,512]{1,0:T(8,128)(2,1)S(1)}, bf16[128,512]{1,0:T(8,128)(2,1)}, u32[]{:S(2)}, u32[]{:S(2)}) collective-permute-start(bf16[128,512]{1,0:T(8,128)(2,1)S(1)} %slice_bitcast_fusion), channel_id=1, source_target_pairs={{1,0},{2,1},{3,2},{4,3},{5,4},{6,5},{7,6},{8,7},{9,8},{10,9},{11,1... | collective-permute-start | bytes 393224 | tf_op jit(solution)/shard_map/ppermute | solution.py:13
  286.1 72.9 %collective-permute-start.2 = (bf16[128,512]{1,0:T(8,128)(2,1)S(1)}, bf16[128,512]{1,0:T(8,128)(2,1)S(1)}, u32[]{:S(2)}, u32[]{:S(2)}) collective-permute-start(bf16[128,512]{1,0:T(8,128)(2,1)S(1)} %slice_bitcast_fusion.2), channel_id=1, source_target_pairs={{1,0},{2,1},{3,2},{4,3},{5,4},{6,5},{7,6},{8,7},{9,8},{10,9},{11,1... | collective-permute-start | bytes 393224 | tf_op jit(solution)/shard_map/ppermute | solution.py:13
  288.8 68.6 %copy-start.20 = (bf16[1,256,512]{2,1,0:T(8,128)(2,1)S(1)}, bf16[1,256,512]{2,1,0:T(8,128)(2,1)}, u32[]{:S(2)}) copy-start(bf16[1,256,512]{2,1,0:T(8,128)(2,1)} %reduce-scatter.11.cloned.1.call-done) | copy-start | bytes 786436
  288.8 153.9 %copy-start.21 = (bf16[1,256,512]{2,1,0:T(8,128)(2,1)S(1)}, bf16[1,256,512]{2,1,0:T(8,128)(2,1)}, u32[]{:S(2)}) copy-start(bf16[1,256,512]{2,1,0:T(8,128)(2,1)} %reduce-scatter.7.cloned.1.call-done) | copy-start | bytes 786436
  (34 other events, 41.3 us)
Sparse Core Ops, SparseCore 0:
  11.6 59.9 all-gather.2
  74.3 48.2 all-gather.4
Sparse Core Ops, SparseCore 1:
  105.9 22.0 reduce-scatter.10
  130.2 23.4 reduce-scatter.6
  275.6 81.7 reduce-scatter.8
  361.1 81.5 reduce-scatter.4
